TPU v7x, 256 devices: a whole 4x4x8 slice. The times are simulated.
256 devices in a mesh: dp: 8 (over y, core), cent: 32 (over x, z).
Axes of the slice: x: 4, y: 4, z: 8, core: 2. Of those that a mesh axis runs over, the one named last changes fastest.
Arguments:
- passages: bfloat16 [32768, 768], P(('dp', 'cent')), may hold values from -10 to 10
- queries: bfloat16 [1024, 768], P(('dp', 'cent')), may hold values from -10 to 10
- init_centroids: float32 [8192, 768], P('cent'), may hold values from -12 to 12
- pattern: int32 [1024, 4], replicated, may hold values from 0 to 255, all different within a row
- positive_offset: int32 [1024], replicated, may hold values from 0 to 127
Outputs:
- centroids: float32 [8192, 768], P('cent')
- loss: float32 [1024], P(('dp', 'cent'))
Inputs may be any that keep to these rules, and one draw needn't show every extreme that they name: `pattern`: each row names 4 different blocks.
All inputs are finite; a program needn't handle non-finite values.
Results may differ from a plain program's by a relative error of at most 0.0055.
Values may be sent and summed in bfloat16 or wider, within the bound.
A program may use at most 64 MiB of HBM per device.

v0:
```python
import jax
import jax.numpy as jnp
from jax import lax
from jax.sharding import PartitionSpec as P

BLOCK = 128
ITERS = 2
sharpness = 0.05
sharpening_factor = 0.05
prior_weight = 1.0


def merged(value, axis, join):
    pieces = jax.tree.map(lambda part: lax.all_gather(part, axis), value)
    head = jax.tree.map(lambda part: part[0], pieces)
    tail = jax.tree.map(lambda part: part[1:], pieces)
    so_far, _ = lax.scan(lambda so_far, section: (join(so_far, section), None), head, tail)
    return so_far


def combine_query(first, second):
    upper = jnp.maximum(first[0], second[0])
    total = first[1] * jnp.exp(first[0] - upper) + second[1] * jnp.exp(second[0] - upper)
    return (upper, total, first[2] + second[2])


def on_device(passages, queries, init_centroids, pattern, positive_offset):
    gathered = lax.all_gather(passages, "cent", axis=0, tiled=True)
    cluster_means = init_centroids
    for step_index in range(ITERS):
        centers_half = cluster_means.astype(jnp.bfloat16)
        cluster_center_norms = jnp.sum(cluster_means * cluster_means, axis=1)
        unnormalized_log_odds = sharpness * (
            2.0 * jnp.dot(gathered, centers_half.T, preferred_element_type=jnp.float32)
            - cluster_center_norms[None, :]
        )
        row_max = lax.pmax(jnp.max(unnormalized_log_odds, axis=1), "cent")
        weights_exp = jnp.exp(unnormalized_log_odds - row_max[:, None])
        row_total = lax.psum(jnp.sum(weights_exp, axis=1), "cent")
        resp = weights_exp / row_total[:, None]
        numer = lax.dot_general(
            resp.astype(jnp.bfloat16),
            gathered,
            (((0,), (0,)), ((), ())),
            preferred_element_type=jnp.float32,
        )
        counts = jnp.sum(resp, axis=0)
        numer, counts = lax.psum((numer, counts), "dp")
        cluster_means = (numer + prior_weight * cluster_means) / (counts[:, None] + prior_weight)
    query_collection = lax.all_gather(queries, ("dp", "cent"), axis=0, tiled=True)
    local_rows = passages.shape[0]
    linear = lax.axis_index(("dp", "cent"))
    first_row = linear * local_rows
    local_blocks = first_row // BLOCK + jnp.arange(local_rows // BLOCK, dtype=jnp.int32)
    paired_entries = jnp.any(pattern[:, :, None] == local_blocks[None, None, :], axis=1)
    allowed = jnp.repeat(paired_entries, BLOCK, axis=1)
    affinity_matrix = (
        jnp.dot(query_collection, passages.T, preferred_element_type=jnp.float32)
        * sharpening_factor
    )
    target_col = pattern[:, 0] * BLOCK + positive_offset - first_row
    columns = jnp.arange(local_rows, dtype=jnp.int32)
    positive = jnp.sum(
        jnp.where(columns[None, :] == target_col[:, None], affinity_matrix, 0.0), axis=1
    )
    local_max = jnp.max(jnp.where(allowed, affinity_matrix, -1e30), axis=1)
    local_total = jnp.sum(
        jnp.where(allowed, jnp.exp(affinity_matrix - local_max[:, None]), 0.0), axis=1
    )
    query_max, query_total, positive_all = merged(
        (local_max, local_total, positive), ("dp", "cent"), combine_query
    )
    whole_loss = jnp.log(query_total) + query_max - positive_all
    own_count = queries.shape[0]
    own_loss = lax.dynamic_slice_in_dim(whole_loss, linear * own_count, own_count, 0)
    return (cluster_means, own_loss)


def solution(mesh):
    placed = (P(("dp", "cent"), None), P(("dp", "cent"), None), P("cent", None), P(), P())
    return jax.shard_map(
        on_device,
        mesh=mesh,
        in_specs=placed,
        out_specs=(P("cent", None), P(("dp", "cent"))),
        check_vma=False,
    )
```

profile of v0, /device:TPU:2, one launch (start us, length us, event | category | flops | bytes accessed | tf_op | source)
XLA Modules:
  0.0 1376.9 jit_solution(4740807136776224495)
XLA Ops:
  8.7 108.5 %all-gather.18.cloned.1.call-done = bf16[256,4,768]{2,1,0:T(4,128)(2,1)} async-done(((bf16[1,4,768]{2,1,0:T(4,128)(2,1)}), bf16[256,4,768]{2,1,0:T(4,128)(2,1)}) %all-gather.18.cloned.1.call-update) | async-done | bytes 1572880 | tf_op jit(solution)/shard_map/all_gather | solution.py:50
  117.2 2.7 reshape.42
  120.0 2.2 select_reduce_fusion.2
  123.0 1.4 select_reduce_fusion
  125.8 97.7 %all-gather.12.cloned.1.call-done = f32[262144]{0:T(1024)} async-done(((f32[1024]{0:T(1024)}), f32[262144]{0:T(1024)}) %all-gather.12.cloned.1.call-update) | async-done | bytes 1048592 | tf_op jit(solution)/shard_map/all_gather | solution.py:14
  223.4 1.3 slice.37
  224.9 103.3 %all-gather.14.cloned.1.call-done = f32[262144]{0:T(1024)} async-done(((f32[1024]{0:T(1024)}), f32[262144]{0:T(1024)}) %all-gather.14.cloned.1.call-update) | async-done | bytes 1048592 | tf_op jit(solution)/shard_map/all_gather | solution.py:14
  328.2 1.3 slice.38
  329.5 1.1 reshape.39
  330.6 102.2 %all-gather.16.cloned.1.call-done = f32[262144]{0:T(1024)} async-done(((f32[1024]{0:T(1024)}), f32[262144]{0:T(1024)}) %all-gather.16.cloned.1.call-update) | async-done | bytes 1048592 | tf_op jit(solution)/shard_map/all_gather | solution.py:14
  432.8 1.3 slice.39
  434.1 1.1 reshape.40
  435.2 218.6 %while.14 = (s32[]{:T(128)}, f32[1024]{0:T(1024)S(1)}, f32[1024]{0:T(1024)S(1)}, f32[1024]{0:T(1024)S(1)}, f32[255,1024]{1,0:T(8,128)S(1)}, /*index=5*/f32[255,1024]{1,0:T(8,128)}, f32[255,1024]{1,0:T(8,128)}, s32[]{:T(128)}) while((s32[]{:T(128)}, f32[1024]{0:T(1024)S(1)}, f32[1024]{0:T(1024)S(1)}, f32[1024]{0:T(1024)S(1)}, ...), condition=%wide.region_21.22_spmd, body=%wide.region_20.21_spmd.sunk | while | flops 7170 | bytes 61541 | solution.py:17
  435.3 0.8 constant_dynamic-slice_fusion.5
  436.1 0.8 constant_dynamic-slice_fusion.5
  445.5 0.8 constant_dynamic-slice_fusion.5
  446.4 0.8 constant_dynamic-slice_fusion.5
  447.3 0.8 constant_dynamic-slice_fusion.5
  452.4 0.8 constant_dynamic-slice_fusion.5
  455.8 0.8 constant_dynamic-slice_fusion.5
  460.1 0.8 constant_dynamic-slice_fusion.5
  463.6 0.8 constant_dynamic-slice_fusion.5
  466.1 0.8 constant_dynamic-slice_fusion.5
  467.0 0.8 constant_dynamic-slice_fusion.5
  484.1 0.8 constant_dynamic-slice_fusion.5
  485.0 0.8 constant_dynamic-slice_fusion.5
  490.1 0.8 constant_dynamic-slice_fusion.5
  491.0 0.8 constant_dynamic-slice_fusion.5
  491.9 0.8 constant_dynamic-slice_fusion.5
  493.6 0.8 constant_dynamic-slice_fusion.5
  495.3 0.8 constant_dynamic-slice_fusion.5
  496.2 0.8 constant_dynamic-slice_fusion.5
  497.0 0.8 constant_dynamic-slice_fusion.5
  499.6 0.8 constant_dynamic-slice_fusion.5
  502.2 0.8 constant_dynamic-slice_fusion.5
  503.0 0.8 constant_dynamic-slice_fusion.5
  503.9 0.8 constant_dynamic-slice_fusion.5
  504.7 0.8 constant_dynamic-slice_fusion.5
  505.6 0.8 constant_dynamic-slice_fusion.5
  507.3 0.8 constant_dynamic-slice_fusion.5
  511.6 0.8 constant_dynamic-slice_fusion.5
  512.5 0.8 constant_dynamic-slice_fusion.5
  513.3 0.8 constant_dynamic-slice_fusion.5
  515.9 0.8 constant_dynamic-slice_fusion.5
  516.8 0.8 constant_dynamic-slice_fusion.5
  517.6 0.8 constant_dynamic-slice_fusion.5
  654.5 6.7 fusion.18
  661.1 130.3 %pmax.14 = f32[4096]{0:T(1024)S(1)} all-reduce(f32[4096]{0:T(1024)S(1)} %get-tuple-element.66), channel_id=1, replica_groups=mesh['dp'=8,'cent'=32] {'cent'}, use_global_device_ids=true, to_apply=%region_2.0 | all-reduce | flops 4096 | bytes 32768 | tf_op jit(solution)/shard_map/pmax | solution.py:37
  791.4 2.8 fusion.5
  794.2 137.7 %psum.42 = f32[4096]{0:T(1024)S(1)} all-reduce(f32[4096]{0:T(1024)S(1)} %fusion.5), channel_id=1, replica_groups=mesh['dp'=8,'cent'=32] {'cent'}, use_global_device_ids=true, to_apply=%region_4.0 | all-reduce | flops 4096 | bytes 32768 | tf_op jit(solution)/shard_map/psum | solution.py:39
  931.8 6.8 fusion.10
  938.7 3.0 fusion.14
  941.7 12.4 psum.44
  954.1 57.1 %all-reduce.3.cloned.1.call-done = f32[256,768]{1,0:T(8,128)} async-done(((f32[256,768]{1,0:T(8,128)}), f32[256,768]{1,0:T(8,128)}) %all-reduce.3.cloned.1.call-update) | async-done | bytes 786448 | tf_op jit(solution)/shard_map/psum | solution.py:48
  1011.3 1.4 multiply_reduce_fusion
  1012.6 6.7 fusion.19
  1019.3 131.0 %pmax.15 = f32[4096]{0:T(1024)S(1)} all-reduce(f32[4096]{0:T(1024)S(1)} %get-tuple-element.68), channel_id=1, replica_groups=mesh['dp'=8,'cent'=32] {'cent'}, use_global_device_ids=true, to_apply=%region_10.0 | all-reduce | flops 4096 | bytes 32768 | tf_op jit(solution)/shard_map/pmax | solution.py:37
  1150.3 2.8 fusion.6
  1153.1 137.9 %psum.45 = f32[4096]{0:T(1024)S(1)} all-reduce(f32[4096]{0:T(1024)S(1)} %fusion.6), channel_id=1, replica_groups=mesh['dp'=8,'cent'=32] {'cent'}, use_global_device_ids=true, to_apply=%region_12.0 | all-reduce | flops 4096 | bytes 32768 | tf_op jit(solution)/shard_map/psum | solution.py:39
  1291.0 6.8 fusion.8
  1297.8 3.0 fusion.12
  1300.8 12.4 psum.47
  1313.2 54.7 %all-reduce.5.cloned.1.call-done = f32[256,768]{1,0:T(8,128)} async-done(((f32[256,768]{1,0:T(8,128)}), f32[256,768]{1,0:T(8,128)}) %all-reduce.5.cloned.1.call-update) | async-done | bytes 786448 | tf_op jit(solution)/shard_map/psum | solution.py:48
  1367.9 2.1 add_divide_fusion
  (1021 shorter events, 187.0 us)
Async XLA Ops:
  7.2 115.8 %copy-start.1 = (s32[1024]{0:T(1024)S(1)}, s32[1024]{0:T(1024)}, u32[]{:S(2)}) copy-start(s32[1024]{0:T(1024)} %param.11) | copy-start | bytes 12292
  7.2 118.5 %copy-start = (f32[256,768]{1,0:T(8,128)S(1)}, f32[256,768]{1,0:T(8,128)}, u32[]{:S(2)}) copy-start(f32[256,768]{1,0:T(8,128)} %param.9) | copy-start | bytes 2359300
  7.2 110.0 %all-gather.18.cloned.1.call-start = ((), (), s32[]{:S(2)}) async-start(), calls=%async_computation.6 | async-start | bytes 1579008 | tf_op jit(solution)/shard_map/all_gather | solution.py:50
  7.9 215.5 %all-gather.12.cloned.1.call-start = ((), (), s32[]{:S(2)}) async-start(), calls=%async_computation.3 | async-start | bytes 1052672 | tf_op jit(solution)/shard_map/all_gather | solution.py:14
  122.2 206.0 %all-gather.14.cloned.1.call-start = ((), (), s32[]{:S(2)}) async-start(), calls=%async_computation.4 | async-start | bytes 1052672 | tf_op jit(solution)/shard_map/all_gather | solution.py:14
  124.4 308.4 %all-gather.16.cloned.1.call-start = ((), (), s32[]{:S(2)}) async-start(), calls=%async_computation.5 | async-start | bytes 1052672 | tf_op jit(solution)/shard_map/all_gather | solution.py:14
  125.0 529.4 %all-gather.10.cloned.1.call-start = ((), (), s32[]{:S(2)}) async-start(), calls=%async_computation | async-start | bytes 6488064 | tf_op jit(solution)/shard_map/all_gather | solution.py:28
  125.6 885.7 %all-reduce.3.cloned.1.call-start = ((), (), s32[]{:S(2)}) async-start(), calls=%async_computation.1 | async-start | bytes 1572864 | tf_op jit(solution)/shard_map/psum | solution.py:48
  224.9 210.3 %slice-start = ((f32[262144]{0:T(1024)}), f32[1024]{0:T(1024)S(1)}, s32[]{:S(2)}) async-start(f32[262144]{0:T(1024)} %all-gather.12.cloned.1.call-done), calls=%async_computation.7 | async-start | bytes 8192 | tf_op jit(solution)/shard_map/slice | solution.py:15
  328.2 107.0 %slice-start.1 = ((f32[262144]{0:T(1024)}), f32[1024]{0:T(1024)S(1)}, s32[]{:S(2)}) async-start(f32[262144]{0:T(1024)} %all-gather.14.cloned.1.call-done), calls=%async_computation.8 | async-start | bytes 8192 | tf_op jit(solution)/shard_map/slice | solution.py:15
  432.8 2.4 slice-start.2
  938.7 429.2 %all-reduce.5.cloned.1.call-start = ((), (), s32[]{:S(2)}) async-start(), calls=%async_computation.2 | async-start | bytes 1572864 | tf_op jit(solution)/shard_map/psum | solution.py:48
Sparse Core Ops, SparseCore 0:
  11.6 105.6 all-gather.17
  122.3 101.0 all-gather.11
  227.2 100.9 all-gather.13
  331.8 100.9 all-gather.15
  435.2 86.4 all-gather.9
  938.8 72.4 all-reduce.2
  1297.9 69.9 all-reduce.4
where the time goes:
time: 1400 us; the launch traced here: 1380 us
  blocking collectives  562 us (40%)
  waiting for transfers between devices  525 us (38%)
  local copies, waits for them, and re-layouts  214 us (15%)
  matrix products  29.1 us (2%)
  other arithmetic  22.3 us (2%)
  between operations  14.2 us (1%)
    all_gather x3, waiting for transfers between devices, merged(): pieces = jax.tree.map(lambda part: lax.all_gather(part, axis), value)  303 us
    psum x2, blocking collectives, on_device(): row_total = lax.psum(jnp.sum(weights_exp, axis=1), 'cent')  276 us
    pmax x2, blocking collectives, on_device(): row_max = lax.pmax(jnp.max(unnormalized_log_odds, axis=1), 'cent')  261 us
    dynamic_slice x510, local copies, waits for them, and re-layouts, merged(): lax.scan(lambda so_far, section: (join(so_far, section), None), head, tail)  205 us
    psum x2, waiting for transfers between devices, on_device(): numer, counts = lax.psum((numer, counts), 'dp')  112 us
    all_gather x1, waiting for transfers between devices, on_device(): lax.all_gather(queries, ('dp', 'cent'), axis=0, tiled=True)  109 us
  transfers between devices with their start and end apart: 7, of which 6 were waited for; matrix products, arithmetic and copies ran while one was open for 16% of the time, Pallas kernels for 0%

commit v1 on v0

--- a/solution.py
+++ b/solution.py
@@ -47,7 +47,10 @@
         counts = jnp.sum(resp, axis=0)
         numer, counts = lax.psum((numer, counts), "dp")
         cluster_means = (numer + prior_weight * cluster_means) / (counts[:, None] + prior_weight)
-    query_collection = lax.all_gather(queries, ("dp", "cent"), axis=0, tiled=True)
+    query_collection = jnp.concatenate(
+        lax.all_to_all(jnp.stack([queries] * lax.axis_size(("dp", "cent"))), ("dp", "cent"), 0, 0),
+        axis=0,
+    )
     local_rows = passages.shape[0]
     linear = lax.axis_index(("dp", "cent"))
     first_row = linear * local_rows

time: 1400 us -> 1340 us (0.957)
  waiting for transfers between devices: 525 us -> 455 us
  starting transfers between devices: 0.28 us -> 14.9 us
    all_gather x1 -> x0, waiting for transfers between devices: 109 us -> none  [on_device(): lax.all_gather(queries, ('dp', 'cent'), axis=0, tiled=True)]
    all_to_all x0 -> x1, waiting for transfers between devices: none -> 42.4 us  [on_device(): lax.all_to_all(jnp.stack([queries] * lax.axis_size(('dp', 'cent'))), ('dp...]
    all_to_all x0 -> x1, starting transfers between devices: none -> 14.7 us  [on_device(): lax.all_to_all(jnp.stack([queries] * lax.axis_size(('dp', 'cent'))), ('dp...]
  transfers between devices with their start and end apart: 7 -> 7, of which waited for: 6 -> 6; matrix products, arithmetic and copies ran while one was open for 16% -> 17% of each run, Pallas kernels for 0% -> 0%
where the time goes in v1:
time: 1340 us; the launch traced here: 1320 us
  blocking collectives  562 us (42%)
  waiting for transfers between devices  455 us (34%)
  local copies, waits for them, and re-layouts  215 us (16%)
  matrix products  29.6 us (2%)
  other arithmetic  20.8 us (2%)
  starting transfers between devices  14.9 us (1%)
  between operations  14.2 us (1%)
    all_gather x3, waiting for transfers between devices, merged(): pieces = jax.tree.map(lambda part: lax.all_gather(part, axis), value)  299 us
    psum x2, blocking collectives, on_device(): row_total = lax.psum(jnp.sum(weights_exp, axis=1), 'cent')  276 us
    pmax x2, blocking collectives, on_device(): row_max = lax.pmax(jnp.max(unnormalized_log_odds, axis=1), 'cent')  261 us
    dynamic_slice x510, local copies, waits for them, and re-layouts, merged(): lax.scan(lambda so_far, section: (join(so_far, section), None), head, tail)  205 us
    psum x2, waiting for transfers between devices, on_device(): numer, counts = lax.psum((numer, counts), 'dp')  112 us
    all_to_all x1, waiting for transfers between devices, on_device(): lax.all_to_all(jnp.stack([queries] * lax.axis_size(('dp', 'cent'))), ('dp...  42.4 us
  transfers between devices with their start and end apart: 7, of which 6 were waited for; matrix products, arithmetic and copies ran while one was open for 17% of the time, Pallas kernels for 0%

profile of v1, /device:TPU:2, one launch (start us, length us, event | category | flops | bytes accessed | tf_op | source)
XLA Modules:
  0.0 1320.8 jit_solution(7963242228436642097)
XLA Ops:
  7.2 2.3 stack.2
  9.5 14.7 %all-to-all-start = ((bf16[256,4,768]{2,1,0:T(4,128)(2,1)}), bf16[256,4,768]{2,1,0:T(4,128)(2,1)S(1)}, u32[]{:S(2)}, u32[]{:S(2)}) async-start(bf16[256,4,768]{2,1,0:T(4,128)(2,1)} %stack.2), calls=%async_computation | async-start | bytes 3145728 | tf_op jit(solution)/shard_map/all_to_all | solution.py:51
  24.3 42.4 %all-to-all-done = bf16[256,4,768]{2,1,0:T(4,128)(2,1)S(1)} async-done(((bf16[256,4,768]{2,1,0:T(4,128)(2,1)}), bf16[256,4,768]{2,1,0:T(4,128)(2,1)S(1)}, u32[]{:S(2)}, u32[]{:S(2)}) %all-to-all-start) | async-done | bytes 1572896 | tf_op jit(solution)/shard_map/all_to_all | solution.py:51
  66.7 1.3 reshape.34
  68.1 2.7 select_reduce_fusion.2
  70.8 1.4 select_reduce_fusion
  73.8 93.5 %all-gather.10.cloned.1.call-done = f32[262144]{0:T(1024)} async-done(((f32[1024]{0:T(1024)}), f32[262144]{0:T(1024)}) %all-gather.10.cloned.1.call-update) | async-done | bytes 1048592 | tf_op jit(solution)/shard_map/all_gather | solution.py:14
  167.3 1.3 slice.37
  168.7 103.3 %all-gather.12.cloned.1.call-done = f32[262144]{0:T(1024)} async-done(((f32[1024]{0:T(1024)}), f32[262144]{0:T(1024)}) %all-gather.12.cloned.1.call-update) | async-done | bytes 1048592 | tf_op jit(solution)/shard_map/all_gather | solution.py:14
  272.0 1.3 slice.38
  273.3 1.1 reshape.45
  274.4 102.3 %all-gather.14.cloned.1.call-done = f32[262144]{0:T(1024)} async-done(((f32[1024]{0:T(1024)}), f32[262144]{0:T(1024)}) %all-gather.14.cloned.1.call-update) | async-done | bytes 1048592 | tf_op jit(solution)/shard_map/all_gather | solution.py:14
  376.8 1.3 slice.39
  378.1 1.1 reshape.46
  379.2 218.6 %while.14 = (s32[]{:T(128)}, f32[1024]{0:T(1024)S(1)}, f32[1024]{0:T(1024)S(1)}, f32[1024]{0:T(1024)S(1)}, f32[255,1024]{1,0:T(8,128)S(1)}, /*index=5*/f32[255,1024]{1,0:T(8,128)}, f32[255,1024]{1,0:T(8,128)}, s32[]{:T(128)}) while((s32[]{:T(128)}, f32[1024]{0:T(1024)S(1)}, f32[1024]{0:T(1024)S(1)}, f32[1024]{0:T(1024)S(1)}, ...), condition=%wide.region_21.22_spmd, body=%wide.region_20.21_spmd.sunk | while | flops 7170 | bytes 61541 | solution.py:17
  380.1 0.8 constant_dynamic-slice_fusion.5
  389.5 0.8 constant_dynamic-slice_fusion.5
  390.4 0.8 constant_dynamic-slice_fusion.5
  391.2 0.8 constant_dynamic-slice_fusion.5
  396.4 0.8 constant_dynamic-slice_fusion.5
  399.8 0.8 constant_dynamic-slice_fusion.5
  404.1 0.8 constant_dynamic-slice_fusion.5
  407.5 0.8 constant_dynamic-slice_fusion.5
  410.1 0.8 constant_dynamic-slice_fusion.5
  410.9 0.8 constant_dynamic-slice_fusion.5
  428.1 0.8 constant_dynamic-slice_fusion.5
  429.0 0.8 constant_dynamic-slice_fusion.5
  434.1 0.8 constant_dynamic-slice_fusion.5
  435.0 0.8 constant_dynamic-slice_fusion.5
  435.8 0.8 constant_dynamic-slice_fusion.5
  437.5 0.8 constant_dynamic-slice_fusion.5
  439.3 0.8 constant_dynamic-slice_fusion.5
  440.1 0.8 constant_dynamic-slice_fusion.5
  441.0 0.8 constant_dynamic-slice_fusion.5
  443.6 0.8 constant_dynamic-slice_fusion.5
  446.1 0.8 constant_dynamic-slice_fusion.5
  447.0 0.8 constant_dynamic-slice_fusion.5
  447.8 0.8 constant_dynamic-slice_fusion.5
  448.7 0.8 constant_dynamic-slice_fusion.5
  449.6 0.8 constant_dynamic-slice_fusion.5
  451.3 0.8 constant_dynamic-slice_fusion.5
  455.6 0.8 constant_dynamic-slice_fusion.5
  456.4 0.8 constant_dynamic-slice_fusion.5
  459.9 0.8 constant_dynamic-slice_fusion.5
  460.7 0.8 constant_dynamic-slice_fusion.5
  461.6 0.8 constant_dynamic-slice_fusion.5
  598.4 6.7 fusion.18
  605.1 130.2 %pmax.14 = f32[4096]{0:T(1024)S(1)} all-reduce(f32[4096]{0:T(1024)S(1)} %get-tuple-element.66), channel_id=1, replica_groups=mesh['dp'=8,'cent'=32] {'cent'}, use_global_device_ids=true, to_apply=%region_2.0 | all-reduce | flops 4096 | bytes 32768 | tf_op jit(solution)/shard_map/pmax | solution.py:37
  735.3 2.8 fusion.5
  738.1 137.7 %psum.42 = f32[4096]{0:T(1024)S(1)} all-reduce(f32[4096]{0:T(1024)S(1)} %fusion.5), channel_id=1, replica_groups=mesh['dp'=8,'cent'=32] {'cent'}, use_global_device_ids=true, to_apply=%region_4.0 | all-reduce | flops 4096 | bytes 32768 | tf_op jit(solution)/shard_map/psum | solution.py:39
  875.8 6.8 fusion.10
  882.7 3.0 fusion.14
  885.6 12.4 psum.44
  898.1 57.2 %all-reduce.3.cloned.1.call-done = f32[256,768]{1,0:T(8,128)} async-done(((f32[256,768]{1,0:T(8,128)}), f32[256,768]{1,0:T(8,128)}) %all-reduce.3.cloned.1.call-update) | async-done | bytes 786448 | tf_op jit(solution)/shard_map/psum | solution.py:48
  955.2 1.4 multiply_reduce_fusion
  956.6 6.7 fusion.19
  963.3 131.0 %pmax.15 = f32[4096]{0:T(1024)S(1)} all-reduce(f32[4096]{0:T(1024)S(1)} %get-tuple-element.68), channel_id=1, replica_groups=mesh['dp'=8,'cent'=32] {'cent'}, use_global_device_ids=true, to_apply=%region_10.0 | all-reduce | flops 4096 | bytes 32768 | tf_op jit(solution)/shard_map/pmax | solution.py:37
  1094.3 2.8 fusion.6
  1097.1 137.9 %psum.45 = f32[4096]{0:T(1024)S(1)} all-reduce(f32[4096]{0:T(1024)S(1)} %fusion.6), channel_id=1, replica_groups=mesh['dp'=8,'cent'=32] {'cent'}, use_global_device_ids=true, to_apply=%region_12.0 | all-reduce | flops 4096 | bytes 32768 | tf_op jit(solution)/shard_map/psum | solution.py:39
  1234.9 6.8 fusion.8
  1241.8 3.0 fusion.12
  1244.7 12.4 psum.47
  1257.2 54.7 %all-reduce.5.cloned.1.call-done = f32[256,768]{1,0:T(8,128)} async-done(((f32[256,768]{1,0:T(8,128)}), f32[256,768]{1,0:T(8,128)}) %all-reduce.5.cloned.1.call-update) | async-done | bytes 786448 | tf_op jit(solution)/shard_map/psum | solution.py:48
  1311.8 2.1 add_divide_fusion
  (1025 shorter events, 186.6 us)
Async XLA Ops:
  7.2 17.1 %copy-start.2 = (s32[1024,4]{0,1:T(4,128)S(1)}, s32[1024,4]{0,1:T(4,128)}, u32[]{:S(2)}) copy-start(s32[1024,4]{0,1:T(4,128)} %param.10) | copy-start | bytes 49156
  7.2 60.9 %copy-start.1 = (bf16[128,768]{1,0:T(8,128)(2,1)S(1)}, bf16[128,768]{1,0:T(8,128)(2,1)}, u32[]{:S(2)}) copy-start(bf16[128,768]{1,0:T(8,128)(2,1)} %param.7) | copy-start | bytes 589828
  9.5 61.3 %copy-start.3 = (s32[1024]{0:T(1024)S(1)}, s32[1024]{0:T(1024)}, u32[]{:S(2)}) copy-start(s32[1024]{0:T(1024)} %param.11) | copy-start | bytes 12292
  9.5 64.2 %copy-start = (f32[256,768]{1,0:T(8,128)S(1)}, f32[256,768]{1,0:T(8,128)}, u32[]{:S(2)}) copy-start(f32[256,768]{1,0:T(8,128)} %param.9) | copy-start | bytes 2359300
  9.5 57.2 %all-to-all-start = ((bf16[256,4,768]{2,1,0:T(4,128)(2,1)}), bf16[256,4,768]{2,1,0:T(4,128)(2,1)S(1)}, u32[]{:S(2)}, u32[]{:S(2)}) async-start(bf16[256,4,768]{2,1,0:T(4,128)(2,1)} %stack.2), calls=%async_computation | async-start | bytes 3145728 | tf_op jit(solution)/shard_map/all_to_all | solution.py:51
  24.2 143.1 %all-gather.10.cloned.1.call-start = ((), (), s32[]{:S(2)}) async-start(), calls=%async_computation.4 | async-start | bytes 1052672 | tf_op jit(solution)/shard_map/all_gather | solution.py:14
  70.7 201.3 %all-gather.12.cloned.1.call-start = ((), (), s32[]{:S(2)}) async-start(), calls=%async_computation.5 | async-start | bytes 1052672 | tf_op jit(solution)/shard_map/all_gather | solution.py:14
  72.3 304.5 %all-gather.14.cloned.1.call-start = ((), (), s32[]{:S(2)}) async-start(), calls=%async_computation.6 | async-start | bytes 1052672 | tf_op jit(solution)/shard_map/all_gather | solution.py:14
  73.0 525.4 %all-gather.8.cloned.1.call-start = ((), (), s32[]{:S(2)}) async-start(), calls=%async_computation.1 | async-start | bytes 6488064 | tf_op jit(solution)/shard_map/all_gather | solution.py:28
  73.6 881.6 %all-reduce.3.cloned.1.call-start = ((), (), s32[]{:S(2)}) async-start(), calls=%async_computation.2 | async-start | bytes 1572864 | tf_op jit(solution)/shard_map/psum | solution.py:48
  168.7 210.5 %slice-start = ((f32[262144]{0:T(1024)}), f32[1024]{0:T(1024)S(1)}, s32[]{:S(2)}) async-start(f32[262144]{0:T(1024)} %all-gather.10.cloned.1.call-done), calls=%async_computation.7 | async-start | bytes 8192 | tf_op jit(solution)/shard_map/slice | solution.py:15
  272.0 107.2 %slice-start.1 = ((f32[262144]{0:T(1024)}), f32[1024]{0:T(1024)S(1)}, s32[]{:S(2)}) async-start(f32[262144]{0:T(1024)} %all-gather.12.cloned.1.call-done), calls=%async_computation.8 | async-start | bytes 8192 | tf_op jit(solution)/shard_map/slice | solution.py:15
  376.8 2.4 slice-start.2
  882.6 429.2 %all-reduce.5.cloned.1.call-start = ((), (), s32[]{:S(2)}) async-start(), calls=%async_computation.3 | async-start | bytes 1572864 | tf_op jit(solution)/shard_map/psum | solution.py:48
Sparse Core Ops, SparseCore 0:
  70.9 96.3 all-gather.9
  171.0 100.9 all-gather.11
  275.8 100.9 all-gather.13
  379.2 86.4 all-gather.7
  882.7 72.4 all-reduce.2
  1241.9 69.8 all-reduce.4
